TPU v7x, 32 devices: a whole 2x2x4 slice. The times are simulated.
32 devices in a mesh: groups: 2 (over y), vocab: 4 (over z), req: 4 (over x, core).
Axes of the slice: x: 2, y: 2, z: 4, core: 2. Of those that a mesh axis runs over, the one named last changes fastest.
Arguments:
- last_states: bfloat16 [512, 8192], P('groups', 'req'), parts along dimension 0, may hold values from -300 to 300
- head_weight: bfloat16 [8192, 32000], P('req', 'vocab'), may hold values from -1 to 1
- embed_table: bfloat16 [32000, 8192], P('vocab', 'req'), may hold values from -200 to 200
- norm_gain: bfloat16 [8192], P('req'), may hold values from 0.099609375 to 1.8984375
- qkv_weight: bfloat16 [8192, 10240], P('req', 'vocab'), may hold values from -0.0625 to 0.0625
- active: int32 [512], P('groups'), parts along dimension 0, may hold values 0 or 1
- slot_request: int32 [512], P('groups'), parts along dimension 0, may hold values from 0 to 255, each once
Outputs:
- soft_embed: bfloat16 [512, 8192], P('groups', 'req'), parts along dimension 0
- qkv_out: bfloat16 [512, 10240], P(('groups', 'req'), 'vocab'), parts along dimension 0
There are 2 independent parts, one for each index of `groups`. A program takes and returns all parts, laid end to end along the dimension named above; an argument that names none is the same for every part. Nothing has to cross between parts.
Inputs may be any that keep to these rules, and one draw needn't show every extreme that they name: `slot_request`: each slot serves a different request.
All inputs are finite; a program needn't handle non-finite values.
Results may differ from a plain program's by a relative error of at most 0.006.
Values may be sent and summed in bfloat16 or wider, within the bound.
A program may use at most 192 MiB of HBM per device.

v0:
```python
import jax
import jax.numpy as jnp
from jax import lax
from jax.sharding import PartitionSpec as P

D = 8192


def combined_all(part, axis, combine):
    gathered = jax.tree.map(lambda a: lax.all_gather(a, axis), part)

    def take(source):
        return jax.tree.map(lambda a: lax.dynamic_index_in_dim(a, source, 0, False), gathered)

    return lax.fori_loop(
        1, lax.axis_size(axis), lambda source, state: combine(state, take(source)), take(0)
    )


def combine_pairs(first, second):
    joined_top = jnp.maximum(first[0], second[0])
    joined_total = first[1] * jnp.exp(first[0] - joined_top) + second[1] * jnp.exp(
        second[0] - joined_top
    )
    return (joined_top, joined_total)


def on_device(last_states, head_weight, embed_table, norm_gain, qkv_weight, active, slot_request):
    state_rows = jnp.take(last_states, slot_request, axis=0)
    partial_logits = jnp.dot(state_rows, head_weight, preferred_element_type=jnp.float32)
    logits = lax.psum(partial_logits, "req")
    local_top = jnp.max(logits, axis=1)
    shifted = jnp.exp(logits - local_top[:, None])
    local_total = jnp.sum(shifted, axis=1)
    row_top, row_total = combined_all((local_top, local_total), "vocab", combine_pairs)
    factor = jnp.exp(local_top - row_top) / row_total * active.astype(jnp.float32)
    weights = (shifted * factor[:, None]).astype(jnp.bfloat16)
    partial_embed = jnp.dot(weights, embed_table, preferred_element_type=jnp.float32)
    mixed = lax.psum(partial_embed, "vocab")
    soft_embed = lax.optimization_barrier(mixed.astype(jnp.bfloat16))
    widened = soft_embed.astype(jnp.float32)
    squares = lax.psum(jnp.sum(widened * widened, axis=1), "req")
    inv_rms = lax.rsqrt(squares / D + 1e-05)
    normed = (widened * inv_rms[:, None] * norm_gain.astype(jnp.float32)[None, :]).astype(
        jnp.bfloat16
    )
    projected = lax.psum_scatter(
        jnp.dot(normed, qkv_weight, preferred_element_type=jnp.float32),
        "req",
        scatter_dimension=0,
        tiled=True,
    )
    return (soft_embed, projected.astype(jnp.bfloat16))


def solution(mesh):
    return jax.shard_map(
        on_device,
        mesh=mesh,
        in_specs=(
            P("groups", "req"),
            P("req", "vocab"),
            P("vocab", "req"),
            P("req"),
            P("req", "vocab"),
            P("groups"),
            P("groups"),
        ),
        out_specs=(P("groups", "req"), P(("groups", "req"), "vocab")),
        check_vma=False,
    )
```

profile of v0, /device:TPU:0, one launch (start us, length us, event | category | flops | bytes accessed | tf_op | source)
XLA Modules:
  0.0 353.8 jit_solution(58645093951876428)
XLA Ops:
  7.2 0.0 copy-start
  7.2 0.0 all-reduce.3.cloned.1.call-start
  7.2 0.8 compare_select_fusion
  8.0 0.7 compare_and_fusion
  8.7 1.4 gather_fusion
  10.1 17.3 %fusion.11 = f32[256,8000]{0,1:T(8,128)} fusion(bf16[2048,8000]{0,1:T(8,128)(2,1)} %param.10, bf16[256,2048]{1,0:T(8,128)(2,1)S(1)} %gather_fusion, pred[256]{0:T(512)(128)(4,1)S(1)} %compare_and_fusion), kind=kOutput, calls=%fused_computation.18 | convolution fusion | flops 8389132288 | bytes 42008832 | tf_op jit(solution)/shard_map/dot_general | solution.py:30
  27.4 0.0 all-reduce.3.cloned.1.call-update
  27.4 0.0 reduce-scatter.2.cloned.1.call-start
  27.4 0.6 copy-done.3
  28.1 151.9 %all-reduce.3.cloned.1.call-done = f32[256,8000]{0,1:T(8,128)} async-done(((f32[256,8000]{0,1:T(8,128)}), f32[256,8000]{0,1:T(8,128)}) %all-reduce.3.cloned.1.call-update) | async-done | bytes 8192016 | tf_op jit(solution)/shard_map/psum | solution.py:31
  179.9 4.4 %reduce_max.9 = f32[256]{0:T(256)S(1)} reduce(f32[256,8000]{0,1:T(8,128)} %all-reduce.3.cloned.1.call-done, f32[]{:T(128)} %constant.67.clone.1), dimensions={1}, to_apply=%region_1.2 | reduce | flops 2047744 | bytes 8193028 | tf_op jit(solution)/shard_map/reduce_max | solution.py:32
  184.3 4.5 %fusion = f32[256]{0:T(256)S(1)} fusion(f32[256,8000]{0,1:T(8,128)} %all-reduce.3.cloned.1.call-done, f32[256]{0:T(256)S(1)} %reduce_max.9), kind=kLoop, calls=%fused_computation.6 | loop fusion | flops 4095744 | bytes 8194048 | tf_op jit(solution)/shard_map/reduce_sum | solution.py:34
  188.8 10.9 %all-gather.3 = f32[4,1,256]{2,1,0:T(1,128)S(1)} all-gather(f32[1,1,256]{2,1,0:T(1,128)S(1)} %bitcast.26), channel_id=3, replica_groups=mesh['groups'=2,'vocab'=4,'req'=4] {'vocab'}, dimensions={0}, use_global_device_ids=true | all-gather | bytes 5120 | tf_op jit(solution)/shard_map/all_gather | solution.py:10
  199.7 7.6 %all-gather.2 = f32[4,1,256]{2,1,0:T(1,128)S(1)} all-gather(f32[1,1,256]{2,1,0:T(1,128)S(1)} %bitcast.23), channel_id=2, replica_groups=mesh['groups'=2,'vocab'=4,'req'=4] {'vocab'}, dimensions={0}, use_global_device_ids=true | all-gather | bytes 5120 | tf_op jit(solution)/shard_map/all_gather | solution.py:10
  207.2 0.1 while.17
  207.4 17.2 %fusion.1 = f32[256,2048]{1,0:T(8,128)S(1)} fusion(bf16[8000,2048]{1,0:T(8,128)(2,1)} %param.11, f32[256,8000]{0,1:T(8,128)} %all-reduce.3.cloned.1.call-done, f32[256]{0:T(256)S(1)} %convert_multiply_fusion.2, f32[256]{0:T(256)S(1)} %reduce_max.9), kind=kOutput, calls=%fused_computation.7 | convolution fusion | flops 8394752000 | bytes 43059200 | tf_op jit(solution)/shard_map/dot_general | solution.py:38
  224.6 70.1 %all-reduce.4 = bf16[256,2048]{1,0:T(8,128)(2,1)S(1)} all-reduce(f32[256,2048]{1,0:T(8,128)S(1)} %fusion.1), channel_id=1, replica_groups=mesh['groups'=2,'vocab'=4,'req'=4] {'vocab'}, use_global_device_ids=true, to_apply=%region_5.6 | all-reduce | flops 524288 | bytes 3145728 | tf_op jit(solution)/shard_map/psum | solution.py:39
  294.7 1.0 copy-done.2
  295.7 0.3 fusion.4
  296.0 5.7 %psum.23 = f32[256]{0:T(256)S(1)} all-reduce(f32[256]{0:T(256)S(1)} %fusion.4), channel_id=1, replica_groups=mesh['groups'=2,'vocab'=4,'req'=4] {'req'}, use_global_device_ids=true, to_apply=%region_7.8 | all-reduce | flops 256 | bytes 2048 | tf_op jit(solution)/shard_map/psum | solution.py:42
  301.7 8.8 %fusion.7 = f32[256,2560]{1,0:T(8,128)} fusion(bf16[2048,2560]{1,0:T(8,128)(2,1)} %param.13, bf16[256,2048]{1,0:T(8,128)(2,1)} %copy-done.2, f32[2048]{0:T(1024)S(1)} %convert_element_type.25, f32[256]{0:T(256)S(1)} %add_rsqrt_fusion), kind=kOutput, calls=%fused_computation.15 | convolution fusion | flops 2686451712 | bytes 14164992 | tf_op jit(solution)/shard_map/dot_general | solution.py:48
  310.5 0.0 reduce-scatter.2.cloned.1.call-update
  310.5 34.6 %reduce-scatter.2.cloned.1.call-done = f32[64,2560]{1,0:T(8,128)} async-done(((f32[256,2560]{1,0:T(8,128)}), f32[64,2560]{1,0:T(8,128)}) %reduce-scatter.2.cloned.1.call-update) | async-done | bytes 655376 | tf_op jit(solution)/shard_map/reduce_scatter | solution.py:47
  345.1 1.8 convert_element_type.27
  (21 shorter events, 0.1 us)
Async XLA Ops:
  7.2 1.5 copy-start
  7.2 172.7 %all-reduce.3.cloned.1.call-start = ((), (), s32[]{:S(2)}) async-start(), calls=%async_computation.1 | async-start | bytes 16384000 | tf_op jit(solution)/shard_map/psum | solution.py:31
  27.4 0.7 copy-start.3
  27.4 317.7 %reduce-scatter.2.cloned.1.call-start = ((), (), s32[]{:S(2)}) async-start(), calls=%async_computation.2 | async-start | bytes 3276800 | tf_op jit(solution)/shard_map/reduce_scatter | solution.py:47
  28.1 179.3 %copy-start.4 = (s32[256]{0:T(256)S(1)}, s32[256]{0:T(256)}, u32[]{:S(2)}) copy-start(s32[256]{0:T(256)} %param.14) | copy-start | bytes 3076
  294.7 1.0 copy-start.2
  301.7 45.3 %copy-start.1 = (bf16[256,2048]{1,0:T(8,128)(2,1)S(1)}, bf16[256,2048]{1,0:T(8,128)(2,1)}, u32[]{:S(2)}) copy-start(bf16[256,2048]{1,0:T(8,128)(2,1)} %param.9) | copy-start | bytes 3145732
Sparse Core Ops, SparseCore 0:
  27.5 152.3 all-reduce.2
  310.6 34.4 reduce-scatter.1
where the time goes:
time: 354 us
  waiting for transfers between devices  186 us (53%)
  blocking collectives  94.2 us (27%)
  matrix products  43.3 us (12%)
  between operations  14.1 us (4%)
  other arithmetic  12.5 us (4%)
    psum x1, waiting for transfers between devices, on_device(): logits = lax.psum(partial_logits, 'req')  152 us
    psum x1, blocking collectives, on_device(): mixed = lax.psum(partial_embed, 'vocab')  70.1 us
    reduce_scatter x1, waiting for transfers between devices, on_device(): lax.psum_scatter(jnp.dot(normed, qkv_weight, preferred_element_type=jnp.f...  34.6 us
    all_gather x2, blocking collectives, combined_all(): gathered = jax.tree.map(lambda a: lax.all_gather(a, axis), part)  18.4 us
    dot_general x1, matrix products, on_device(): jnp.dot(state_rows, head_weight, preferred_element_type=jnp.float32)  17.3 us
    dot_general x1, matrix products, on_device(): jnp.dot(weights, embed_table, preferred_element_type=jnp.float32)  17.2 us
    dot_general x1, matrix products, on_device(): jnp.dot(normed, qkv_weight, preferred_element_type=jnp.float32)  8.81 us
  transfers between devices with their start and end apart: 2, of which 2 were waited for; matrix products, arithmetic and copies ran while one was open for 0% of the time, Pallas kernels for 0%

commit v1 on v0

v1 whole, which is shorter than its diff:
```python
import functools

import jax
import jax.numpy as jnp
from jax import lax
from jax.experimental import pallas as pl
from jax.experimental.pallas import tpu as pltpu
from jax.sharding import PartitionSpec as P

D = 8192
MESH = pl.DeviceIdType.MESH
VMEM_LIMIT = 56 * 1024 * 1024


def greet(targets):
    barrier = pltpu.get_barrier_semaphore()
    for target in targets:
        pl.semaphore_signal(barrier, inc=1, device_id=target, device_id_type=MESH)
    pl.semaphore_wait(barrier, len(targets))


def remote(src, dst, send, recv, target):
    return pltpu.make_async_remote_copy(
        src_ref=src, dst_ref=dst, send_sem=send, recv_sem=recv, device_id=target, device_id_type=MESH
    )


def req_position(nx):
    me = lax.axis_index("req")
    chip, core = lax.div(me, 2), lax.rem(me, 2)
    partner = {"req": chip * 2 + (1 - core)}

    def chip_at(d):
        return lax.rem(chip + d, nx)

    def peer(d):
        return {"req": chip_at(d) * 2 + core}

    return me, chip, core, partner, chip_at, peer


def vocab_peers(nz):
    z = lax.axis_index("vocab")
    return z, [{"vocab": lax.rem(z + d, nz)} for d in range(1, nz)]


def weights_kernel(nx, nz, steps, part_ref, active_ref, out_ref, core_buf, own_buf, chip_buf, stats,
                   stats_in, core_send, core_recv, own_sem, chip_send, chip_recv, stat_send, stat_recv,
                   pair_send, pair_recv, gather_send, gather_recv, fwd_send, fwd_recv):
    me, chip, core, partner, chip_at, peer = req_position(nx)
    _, zpeers = vocab_peers(nz)
    own_rows = part_ref.shape[0] // (2 * nx)
    s = own_rows // steps
    lane = lax.broadcasted_iota(jnp.int32, (s, 128), 1)
    greet([partner] + [peer(d) for d in range(1, nx)] + zpeers)

    core_copies, own_copies = [], []
    for j in range(steps):
        core_copies.append([])
        own_copies.append([])
        for d in list(range(1, nx)) + [0]:
            there = pl.multiple_of((chip_at(d) * 2 + 1 - core) * own_rows + j * s, s)
            here = pl.multiple_of((chip_at(d) * 2 + core) * own_rows + j * s, s)
            copy = remote(part_ref.at[pl.ds(there, s)], core_buf.at[j, d], core_send.at[j, d],
                          core_recv.at[j, d], partner)
            local = pltpu.make_async_copy(part_ref.at[pl.ds(here, s)], own_buf.at[j, d], own_sem.at[j, d])
            copy.start()
            local.start()
            core_copies[j].append(copy)
            own_copies[j].append(local)

    chip_copies, stat_copies, gather_copies, fwd_copies = {}, {}, {}, {}

    def reduce_cores(j):
        for i in range(nx):
            d = i + 1 if i < nx - 1 else 0
            own_copies[j][i].wait()
            core_copies[j][i].wait_recv()
            own_buf[j, d] = own_buf[j, d] + core_buf[j, d]
            if d > 0:
                copy = remote(own_buf.at[j, d], chip_buf.at[j, d - 1], chip_send.at[j, d - 1],
                              chip_recv.at[j, d - 1], peer(d))
                copy.start()
                chip_copies[j, d] = copy

    def exponentials(j):
        for d in range(1, nx):
            chip_copies[j, d].wait_recv()
        total = own_buf[j, 0]
        for d in range(1, nx):
            total = total + chip_buf[j, d - 1]
        top = jnp.max(total, axis=1, keepdims=True)
        shifted = jnp.exp(total - top)
        own_buf[j, 0] = shifted
        stats[j] = jnp.where(lane < 64, top, jnp.sum(shifted, axis=1, keepdims=True))
        for i, target in enumerate(zpeers):
            copy = remote(stats.at[j], stats_in.at[j, i], stat_send.at[j, i], stat_recv.at[j, i], target)
            copy.start()
            stat_copies[j, i] = copy

    def rows_of(owner, j):
        return pl.ds(pl.multiple_of(owner * own_rows + j * s, s), s)

    def normalise(j):
        for i in range(nz - 1):
            stat_copies[j, i].wait_recv()
        mine = stats[j]
        my_top, row_total = mine[:, 0:1], mine[:, 64:65]
        row_top = my_top
        for i in range(nz - 1):
            row_top = jnp.maximum(row_top, stats_in[j, i][:, 0:1])
        row_total = row_total * jnp.exp(my_top - row_top)
        for i in range(nz - 1):
            other = stats_in[j, i]
            row_total = row_total + other[:, 64:65] * jnp.exp(other[:, 0:1] - row_top)
        live = active_ref[rows_of(me, j), :][:, 0:1]
        factor = jnp.exp(my_top - row_top) / row_total * live
        mine_rows = out_ref.at[rows_of(me, j)]
        mine_rows[...] = (own_buf[j, 0] * factor).astype(out_ref.dtype)
        for d in range(1, nx):
            copy = remote(mine_rows, mine_rows, gather_send.at[j, d - 1], gather_recv.at[j, d - 1], peer(d))
            copy.start()
            gather_copies[j, d] = copy
        copy = remote(mine_rows, mine_rows, pair_send.at[j], pair_recv.at[j], partner)
        copy.start()
        gather_copies[j, 0] = copy

    def forward(j):
        for d in range(1, nx):
            gather_copies[j, d].wait_recv()
            block = out_ref.at[rows_of(chip_at(nx - d) * 2 + core, j)]
            copy = remote(block, block, fwd_send.at[j, d - 1], fwd_recv.at[j, d - 1], partner)
            copy.start()
            fwd_copies[j, d] = copy

    for t in range(steps + 3):
        if t < steps:
            reduce_cores(t)
        if 0 <= t - 1 < steps:
            exponentials(t - 1)
        if 0 <= t - 2 < steps:
            normalise(t - 2)
        if 0 <= t - 3 < steps:
            forward(t - 3)
    for j in range(steps):
        gather_copies[j, 0].wait_recv()
        for d in range(1, nx):
            fwd_copies[j, d].wait_recv()
    for j in range(steps):
        for copy in core_copies[j]:
            copy.wait_send()
    for group in (chip_copies, stat_copies, gather_copies, fwd_copies):
        for copy in group.values():
            copy.wait_send()


def gathered_weights(part, active, nx, nz):
    rows, words = part.shape
    steps = 4
    s = rows // (2 * nx) // steps
    far = max(nx - 1, 1)
    dma = pltpu.SemaphoreType.DMA
    return pl.pallas_call(
        functools.partial(weights_kernel, nx, nz, steps),
        out_shape=jax.ShapeDtypeStruct((rows, words), jnp.bfloat16),
        in_specs=[pl.BlockSpec(memory_space=pl.ANY), pl.BlockSpec(memory_space=pltpu.VMEM)],
        out_specs=pl.BlockSpec(memory_space=pltpu.VMEM),
        scratch_shapes=[
            pltpu.VMEM((steps, nx, s, words), jnp.float32),
            pltpu.VMEM((steps, nx, s, words), jnp.float32),
            pltpu.VMEM((steps, far, s, words), jnp.float32),
            pltpu.VMEM((steps, s, 128), jnp.float32),
            pltpu.VMEM((steps, nz - 1, s, 128), jnp.float32),
            dma((steps, nx)), dma((steps, nx)), dma((steps, nx)),
            dma((steps, far)), dma((steps, far)),
            dma((steps, nz - 1)), dma((steps, nz - 1)),
            dma((steps,)), dma((steps,)),
            dma((steps, far)), dma((steps, far)),
            dma((steps, far)), dma((steps, far)),
        ],
        compiler_params=pltpu.CompilerParams(
            collective_id=0, has_side_effects=True, vmem_limit_bytes=VMEM_LIMIT
        ),
        name="weights",
    )(part, active)


def embed_kernel(nz, parts, part_ref, out_ref, inbox, send, recv, out_send, out_recv):
    z, zpeers = vocab_peers(nz)
    rows = part_ref.shape[0] // nz
    s = rows // parts
    greet(zpeers)

    def rows_of(owner, h):
        return pl.ds(pl.multiple_of(owner * rows + h * s, s), s)

    copies, gathers = {}, {}
    for h in range(parts):
        for d in range(1, nz):
            copy = remote(part_ref.at[rows_of(lax.rem(z + d, nz), h)], inbox.at[h, d - 1],
                          send.at[h, d - 1], recv.at[h, d - 1], zpeers[d - 1])
            copy.start()
            copies[h, d] = copy
    for h in range(parts):
        total = part_ref[rows_of(z, h), :].astype(jnp.float32)
        for d in range(1, nz):
            copies[h, d].wait_recv()
            total = total + inbox[h, d - 1].astype(jnp.float32)
        block = out_ref.at[rows_of(z, h)]
        block[...] = total.astype(out_ref.dtype)
        for d in range(1, nz):
            copy = remote(block, block, out_send.at[h, d - 1], out_recv.at[h, d - 1], zpeers[d - 1])
            copy.start()
            gathers[h, d] = copy
    for copy in gathers.values():
        copy.wait_recv()
    for copy in list(copies.values()) + list(gathers.values()):
        copy.wait_send()


def summed_embed(part, nz):
    rows, columns = part.shape
    parts = 2
    s = rows // nz // parts
    dma = pltpu.SemaphoreType.DMA
    return pl.pallas_call(
        functools.partial(embed_kernel, nz, parts),
        out_shape=jax.ShapeDtypeStruct((rows, columns), jnp.bfloat16),
        in_specs=[pl.BlockSpec(memory_space=pltpu.VMEM)],
        out_specs=pl.BlockSpec(memory_space=pltpu.VMEM),
        scratch_shapes=[
            pltpu.VMEM((parts, nz - 1, s, columns), jnp.bfloat16),
            dma((parts, nz - 1)), dma((parts, nz - 1)), dma((parts, nz - 1)), dma((parts, nz - 1)),
        ],
        compiler_params=pltpu.CompilerParams(
            collective_id=1, has_side_effects=True, vmem_limit_bytes=VMEM_LIMIT
        ),
        name="embed_sum",
    )(part)


def qkv_kernel(nx, steps, part_ref, squares_ref, out_ref, core_buf, own_buf, chip_out, chip_in, squares_in,
               core_send, core_recv, own_sem, chip_send, chip_recv, sq_send, sq_recv):
    me, chip, core, partner, chip_at, peer = req_position(nx)
    own_rows = part_ref.shape[0] // (2 * nx)
    s = own_rows // steps
    n = 2 * nx
    others = [lax.rem(me + d, n) for d in range(1, n)]
    greet([{"req": other} for other in others])

    core_copies, own_copies = [], []
    for j in range(steps):
        core_copies.append([])
        own_copies.append([])
        for d in list(range(1, nx)) + [0]:
            there = pl.multiple_of((chip_at(d) * 2 + 1 - core) * own_rows + j * s, s)
            here = pl.multiple_of((chip_at(d) * 2 + core) * own_rows + j * s, s)
            copy = remote(part_ref.at[pl.ds(there, s)], core_buf.at[j, d], core_send.at[j, d],
                          core_recv.at[j, d], partner)
            local = pltpu.make_async_copy(part_ref.at[pl.ds(here, s)], own_buf.at[j, d], own_sem.at[j, d])
            copy.start()
            local.start()
            core_copies[j].append(copy)
            own_copies[j].append(local)
    sq_copies = []
    for i, other in enumerate(others):
        block = squares_ref.at[pl.ds(pl.multiple_of(other * own_rows, own_rows), own_rows)]
        copy = remote(block, squares_in.at[i], sq_send.at[i], sq_recv.at[i], {"req": other})
        copy.start()
        sq_copies.append(copy)

    chip_copies = {}
    for j in range(steps):
        for i in range(nx):
            d = i + 1 if i < nx - 1 else 0
            own_copies[j][i].wait()
            core_copies[j][i].wait_recv()
            total = own_buf[j, d] + core_buf[j, d]
            if d > 0:
                chip_out[j, d - 1] = total.astype(chip_out.dtype)
                copy = remote(chip_out.at[j, d - 1], chip_in.at[j, d - 1], chip_send.at[j, d - 1],
                              chip_recv.at[j, d - 1], peer(d))
                copy.start()
                chip_copies[j, d] = copy
            else:
                own_buf[j, 0] = total
    squares = squares_ref[pl.ds(pl.multiple_of(me * own_rows, own_rows), own_rows), :]
    for i, copy in enumerate(sq_copies):
        copy.wait_recv()
        squares = squares + squares_in[i]
    inv_rms = lax.rsqrt(squares[:, 0:1] / D + 1e-05)
    for j in range(steps):
        total = own_buf[j, 0]
        for d in range(1, nx):
            chip_copies[j, d].wait_recv()
            total = total + chip_in[j, d - 1].astype(jnp.float32)
        out_ref[j * s : (j + 1) * s, :] = (total * inv_rms[j * s : (j + 1) * s]).astype(out_ref.dtype)
    for j in range(steps):
        for copy in core_copies[j]:
            copy.wait_send()
    for copy in sq_copies + list(chip_copies.values()):
        copy.wait_send()


def scattered_qkv(part, squares, nx):
    rows, columns = part.shape
    steps = 2
    own = rows // (2 * nx)
    s = own // steps
    far = max(nx - 1, 1)
    dma = pltpu.SemaphoreType.DMA
    return pl.pallas_call(
        functools.partial(qkv_kernel, nx, steps),
        out_shape=jax.ShapeDtypeStruct((own, columns), jnp.bfloat16),
        in_specs=[pl.BlockSpec(memory_space=pl.ANY), pl.BlockSpec(memory_space=pltpu.VMEM)],
        out_specs=pl.BlockSpec(memory_space=pltpu.VMEM),
        scratch_shapes=[
            pltpu.VMEM((steps, nx, s, columns), jnp.float32),
            pltpu.VMEM((steps, nx, s, columns), jnp.float32),
            pltpu.VMEM((steps, far, s, columns), jnp.bfloat16),
            pltpu.VMEM((steps, far, s, columns), jnp.bfloat16),
            pltpu.VMEM((2 * nx - 1, own, 128), jnp.float32),
            dma((steps, nx)), dma((steps, nx)), dma((steps, nx)),
            dma((steps, far)), dma((steps, far)),
            dma((2 * nx - 1,)), dma((2 * nx - 1,)),
        ],
        compiler_params=pltpu.CompilerParams(
            collective_id=2, has_side_effects=True, vmem_limit_bytes=VMEM_LIMIT
        ),
        name="qkv_sum",
    )(part, squares)


def on_device(nx, nz, last_states, head_weight, embed_table, norm_gain, qkv_weight, active, slot_request):
    rows = last_states.shape[0]
    state_rows = jnp.take(last_states, slot_request, axis=0)
    partial_logits = jnp.dot(state_rows, head_weight, preferred_element_type=jnp.float32)
    live = jnp.broadcast_to(active.astype(jnp.float32)[:, None], (rows, 128))
    weights = gathered_weights(partial_logits, live, nx, nz)
    partial_embed = jnp.dot(weights, embed_table, preferred_element_type=jnp.float32)
    soft_embed = summed_embed(partial_embed.astype(jnp.bfloat16), nz)
    widened = soft_embed.astype(jnp.float32)
    squares = jnp.broadcast_to(jnp.sum(widened * widened, axis=1)[:, None], (rows, 128))
    scaled = (widened * norm_gain.astype(jnp.float32)[None, :]).astype(jnp.bfloat16)
    partial_qkv = jnp.dot(scaled, qkv_weight, preferred_element_type=jnp.float32)
    return (soft_embed, scattered_qkv(partial_qkv, squares, nx))


def solution(mesh):
    nx, nz = mesh.shape["req"] // 2, mesh.shape["vocab"]
    return jax.shard_map(
        functools.partial(on_device, nx, nz),
        mesh=mesh,
        in_specs=(
            P("groups", "req"),
            P("req", "vocab"),
            P("vocab", "req"),
            P("req"),
            P("req", "vocab"),
            P("groups"),
            P("groups"),
        ),
        out_specs=(P("groups", "req"), P(("groups", "req"), "vocab")),
        check_vma=False,
    )
```

time: 354 us -> 194 us (0.55)
  waiting for transfers between devices: 186 us -> 0 us
  Pallas kernels: 0 us -> 143 us
  blocking collectives: 94.2 us -> 0 us
  between operations: 14.1 us -> 0.75 us
  other arithmetic: 12.5 us -> 1.07 us
    psum x1 -> x0, waiting for transfers between devices: 152 us -> none  [on_device(): logits = lax.psum(partial_logits, 'req')]
    pallas_call x0 -> x3, Pallas kernels: none -> 143 us  [the longest x1 80.2 us: gathered_weights(): pl.pallas_call(functools.partial(weights_kernel, nx, nz, steps), out_shap...]
    psum x2 -> x0, blocking collectives: 75.8 us -> none  [the longest x1 70.1 us: on_device(): mixed = lax.psum(partial_embed, 'vocab')]
    reduce_scatter x1 -> x0, waiting for transfers between devices: 34.6 us -> none  [on_device(): lax.psum_scatter(jnp.dot(normed, qkv_weight, preferred_element_type=jnp.f...]
    all_gather x2 -> x0, blocking collectives: 18.4 us -> none  [combined_all(): gathered = jax.tree.map(lambda a: lax.all_gather(a, axis), part)]
    reduce_sum x2 -> x1, other arithmetic: 4.75 us -> 0.28 us  [on_device(): jnp.sum(widened * widened, axis=1)[:, None]]
    reduce_max x1 -> x0, other arithmetic: 4.39 us -> none  [on_device(): local_top = jnp.max(logits, axis=1)]
  transfers between devices with their start and end apart: 2 -> 0, of which waited for: 2 -> 0; matrix products, arithmetic and copies ran while one was open for 0% -> 0% of each run, Pallas kernels for 0% -> 0%
where the time goes in v1:
time: 194 us
  Pallas kernels  143 us (74%)
  matrix products  42.9 us (22%)
  local copies, waits for them, and re-layouts  6.05 us (3%)
    pallas_call x1, Pallas kernels, gathered_weights(): pl.pallas_call(functools.partial(weights_kernel, nx, nz, steps), out_shap...  80.2 us
    pallas_call x1, Pallas kernels, summed_embed(): pl.pallas_call(functools.partial(embed_kernel, nz, parts), out_shape=jax....  49.1 us
    dot_general x1, matrix products, on_device(): jnp.dot(state_rows, head_weight, preferred_element_type=jnp.float32)  17.3 us
    dot_general x1, matrix products, on_device(): jnp.dot(weights, embed_table, preferred_element_type=jnp.float32)  16.8 us
    pallas_call x1, Pallas kernels, scattered_qkv(): pl.pallas_call(functools.partial(qkv_kernel, nx, steps), out_shape=jax.Sh...  13.7 us
    dot_general x1, matrix products, on_device(): jnp.dot(scaled, qkv_weight, preferred_element_type=jnp.float32)  8.81 us

profile of v1, /device:TPU:0, one launch (start us, length us, event | category | flops | bytes accessed | tf_op | source)
XLA Modules:
  0.0 193.8 jit_solution(17111238595488220937)
XLA Ops:
  0.6 0.0 copy-start
  0.6 0.0 copy-start.4
  0.7 0.8 compare_select_fusion
  1.4 0.4 copy-done
  1.9 1.4 gather_fusion
  3.2 0.0 copy-done.4
  3.3 0.0 copy-start.5
  3.3 17.3 %fusion.5.part_ref = f32[256,8000]{1,0:T(8,128)} fusion(bf16[2048,8000]{0,1:T(8,128)(2,1)} %param.8, bf16[256,2048]{1,0:T(8,128)(2,1)S(1)} %gather_fusion, pred[256]{0:T(512)(128)(4,1)S(1)} %compare_and_fusion), kind=kOutput, calls=%fused_computation.8 | convolution fusion | flops 8389132288 | bytes 42008832 | tf_op jit(solution)/shard_map/dot_general | solution.py:337
  20.5 0.0 copy-done.5
  20.6 0.8 broadcast_in_dim.28.active_ref
  21.3 80.2 %weights.1 = bf16[256,8000]{1,0:T(8,128)(2,1)} custom-call(f32[256,8000]{1,0:T(8,128)} %fusion.5.part_ref, f32[256,128]{1,0:T(8,128)} %broadcast_in_dim.28.active_ref), custom_call_target="tpu_custom_call" | custom-call | tf_op jit(solution)/shard_map/weights/pallas_call | solution.py:163
  101.5 0.0 copy-start.3
  101.5 16.8 %convolution_convert_fusion.part_ref = bf16[256,2048]{1,0:T(8,128)(2,1)} fusion(bf16[256,8000]{1,0:T(8,128)(2,1)} %weights.1, bf16[8000,2048]{1,0:T(8,128)(2,1)} %param.9), kind=kOutput, calls=%fused_computation.3 | convolution fusion | flops 8389132288 | bytes 37912576 | tf_op jit(solution)/shard_map/dot_general | solution.py:340
  118.3 49.1 %embed_sum.1 = bf16[256,2048]{1,0:T(8,128)(2,1)} custom-call(bf16[256,2048]{1,0:T(8,128)(2,1)} %convolution_convert_fusion.part_ref), custom_call_target="tpu_custom_call" | custom-call | tf_op jit(solution)/shard_map/embed_sum/pallas_call | solution.py:226
  167.4 0.0 copy-done.3
  167.4 0.0 copy-start.2
  167.5 0.0 copy-start.1
  167.5 8.8 %fusion.2.part_ref = f32[256,2560]{1,0:T(8,128)} fusion(bf16[2048,2560]{1,0:T(8,128)(2,1)} %param.11, bf16[256,2048]{1,0:T(8,128)(2,1)} %embed_sum.1, f32[2048]{0:T(1024)S(1)} %convert_element_type.18), kind=kOutput, calls=%fused_computation.6 | convolution fusion | flops 2685927424 | bytes 14163968 | tf_op jit(solution)/shard_map/dot_general | solution.py:345
  176.3 0.3 fusion.1
  176.6 0.8 broadcast_in_dim.29.squares_ref
  177.3 13.7 %qkv_sum.1 = bf16[64,2560]{1,0:T(8,128)(2,1)} custom-call(f32[256,2560]{1,0:T(8,128)} %fusion.2.part_ref, f32[256,128]{1,0:T(8,128)} %broadcast_in_dim.29.squares_ref), custom_call_target="tpu_custom_call" | custom-call | tf_op jit(solution)/shard_map/qkv_sum/pallas_call | solution.py:312
  191.1 1.0 copy.11
  192.0 1.7 copy.12
  193.8 0.0 copy-done.1
  (5 shorter events, 0.0 us)
Async XLA Ops:
  0.6 1.2 copy-start
  0.6 2.6 %copy-start.4 = (s32[256]{0:T(256)S(1)}, s32[256]{0:T(256)}, u32[]{:S(2)}) copy-start(s32[256]{0:T(256)} %param.13) | copy-start | bytes 3076
  3.3 17.3 %copy-start.5 = (s32[256]{0:T(256)S(1)}, s32[256]{0:T(256)}, u32[]{:S(2)}) copy-start(s32[256]{0:T(256)} %param.12) | copy-start | bytes 3076
  101.5 66.0 %copy-start.3 = (bf16[2048]{0:T(1024)(128)(2,1)S(1)}, bf16[2048]{0:T(1024)(128)(2,1)}, u32[]{:S(2)}) copy-start(bf16[2048]{0:T(1024)(128)(2,1)} %param.10) | copy-start | bytes 12292
  167.4 8.8 %copy-start.2 = (bf16[256,2048]{1,0:T(8,128)(2,1)S(1)}, bf16[256,2048]{1,0:T(8,128)(2,1)}, u32[]{:S(2)}) copy-start(bf16[256,2048]{1,0:T(8,128)(2,1)} %embed_sum.1) | copy-start | bytes 3145732
  167.5 26.3 %copy-start.1 = (bf16[256,2048]{1,0:T(8,128)(2,1)S(1)}, bf16[256,2048]{1,0:T(8,128)(2,1)}, u32[]{:S(2)}) copy-start(bf16[256,2048]{1,0:T(8,128)(2,1)} %param.7) | copy-start | bytes 3145732

commit v2 on v1

--- a/solution.py
+++ b/solution.py
@@ -9,7 +9,7 @@
 
 D = 8192
 MESH = pl.DeviceIdType.MESH
-VMEM_LIMIT = 56 * 1024 * 1024
+VMEM_LIMIT = 60 * 1024 * 1024
 
 
 def greet(targets):
@@ -44,13 +44,16 @@
     return z, [{"vocab": lax.rem(z + d, nz)} for d in range(1, nz)]
 
 
-def weights_kernel(nx, nz, steps, part_ref, active_ref, out_ref, core_buf, own_buf, chip_buf, stats,
-                   stats_in, core_send, core_recv, own_sem, chip_send, chip_recv, stat_send, stat_recv,
-                   pair_send, pair_recv, gather_send, gather_recv, fwd_send, fwd_recv):
+def mixed_kernel(nx, nz, steps, part_ref, active_ref, embed_ref, out_ref, core_buf, own_buf, chip_buf,
+                 weights, table, mixed, inbox, stats, stats_in, table_sem, core_send, core_recv, own_sem,
+                 chip_send, chip_recv, stat_send, stat_recv, pair_send, pair_recv, gather_send,
+                 gather_recv, fwd_send, fwd_recv, mix_send, mix_recv, out_send, out_recv):
     me, chip, core, partner, chip_at, peer = req_position(nx)
-    _, zpeers = vocab_peers(nz)
+    z, zpeers = vocab_peers(nz)
     own_rows = part_ref.shape[0] // (2 * nx)
     s = own_rows // steps
+    piece = 2 * nx * s // nz
+    tile = 256
     lane = lax.broadcasted_iota(jnp.int32, (s, 128), 1)
     greet([partner] + [peer(d) for d in range(1, nx)] + zpeers)
 
@@ -68,8 +71,11 @@
             local.start()
             core_copies[j].append(copy)
             own_copies[j].append(local)
+    table_copy = pltpu.make_async_copy(embed_ref, table, table_sem)
+    table_copy.start()
 
     chip_copies, stat_copies, gather_copies, fwd_copies = {}, {}, {}, {}
+    mix_copies, out_copies = {}, {}
 
     def reduce_cores(j):
         for i in range(nx):
@@ -98,8 +104,8 @@
             copy.start()
             stat_copies[j, i] = copy
 
-    def rows_of(owner, j):
-        return pl.ds(pl.multiple_of(owner * own_rows + j * s, s), s)
+    def rows_of(owner):
+        return pl.ds(pl.multiple_of(owner * s, s), s)
 
     def normalise(j):
         for i in range(nz - 1):
@@ -113,10 +119,10 @@
         for i in range(nz - 1):
             other = stats_in[j, i]
             row_total = row_total + other[:, 64:65] * jnp.exp(other[:, 0:1] - row_top)
-        live = active_ref[rows_of(me, j), :][:, 0:1]
+        live = active_ref[pl.ds(pl.multiple_of(me * own_rows + j * s, s), s), :][:, 0:1]
         factor = jnp.exp(my_top - row_top) / row_total * live
-        mine_rows = out_ref.at[rows_of(me, j)]
-        mine_rows[...] = (own_buf[j, 0] * factor).astype(out_ref.dtype)
+        mine_rows = weights.at[j, rows_of(me)]
+        mine_rows[...] = (own_buf[j, 0] * factor).astype(weights.dtype)
         for d in range(1, nx):
             copy = remote(mine_rows, mine_rows, gather_send.at[j, d - 1], gather_recv.at[j, d - 1], peer(d))
             copy.start()
@@ -128,115 +134,114 @@
     def forward(j):
         for d in range(1, nx):
             gather_copies[j, d].wait_recv()
-            block = out_ref.at[rows_of(chip_at(nx - d) * 2 + core, j)]
+            block = weights.at[j, rows_of(chip_at(nx - d) * 2 + core)]
             copy = remote(block, block, fwd_send.at[j, d - 1], fwd_recv.at[j, d - 1], partner)
             copy.start()
             fwd_copies[j, d] = copy
 
-    for t in range(steps + 3):
-        if t < steps:
-            reduce_cores(t)
-        if 0 <= t - 1 < steps:
-            exponentials(t - 1)
-        if 0 <= t - 2 < steps:
-            normalise(t - 2)
-        if 0 <= t - 3 < steps:
-            forward(t - 3)
-    for j in range(steps):
+    def piece_of(owner):
+        return pl.ds(pl.multiple_of(owner * piece, piece), piece)
+
+    def mix(j):
+        if j == 0:
+            table_copy.wait()
         gather_copies[j, 0].wait_recv()
         for d in range(1, nx):
             fwd_copies[j, d].wait_recv()
+
+        @pl.loop(0, table.shape[1] // tile)
+        def _(c):
+            columns = pl.ds(pl.multiple_of(c * tile, tile), tile)
+            mixed[j, :, columns] = jnp.dot(
+                weights[j], table[:, columns], preferred_element_type=jnp.float32
+            ).astype(mixed.dtype)
+
+        for d in range(1, nz):
+            copy = remote(mixed.at[j, piece_of(lax.rem(z + d, nz))], inbox.at[j, d - 1],
+                          mix_send.at[j, d - 1], mix_recv.at[j, d - 1], zpeers[d - 1])
+            copy.start()
+            mix_copies[j, d] = copy
+
+    def gather_mixed(j):
+        total = mixed[j, piece_of(z), :].astype(jnp.float32)
+        for d in range(1, nz):
+            mix_copies[j, d].wait_recv()
+            total = total + inbox[j, d - 1].astype(jnp.float32)
+        block = out_ref.at[j, piece_of(z)]
+        block[...] = total.astype(out_ref.dtype)
+        for d in range(1, nz):
+            copy = remote(block, block, out_send.at[j, d - 1], out_recv.at[j, d - 1], zpeers[d - 1])
+            copy.start()
+            out_copies[j, d] = copy
+
+    for t in range(min(2, steps)):
+        reduce_cores(t)
+    for t in range(steps):
+        exponentials(t)
+        if t >= 2:
+            gather_mixed(t - 2)
+        normalise(t)
+        if t + 2 < steps:
+            reduce_cores(t + 2)
+        if t >= 1:
+            forward(t - 1)
+            mix(t - 1)
+    if steps >= 2:
+        gather_mixed(steps - 2)
+    forward(steps - 1)
+    mix(steps - 1)
+    gather_mixed(steps - 1)
+    for copy in out_copies.values():
+        copy.wait_recv()
     for j in range(steps):
         for copy in core_copies[j]:
             copy.wait_send()
-    for group in (chip_copies, stat_copies, gather_copies, fwd_copies):
+    for group in (chip_copies, stat_copies, gather_copies, fwd_copies, mix_copies, out_copies):
         for copy in group.values():
             copy.wait_send()
 
 
-def gathered_weights(part, active, nx, nz):
+def expected_embedding(part, active, embed_table, nx, nz, steps):
     rows, words = part.shape
-    steps = 4
+    width = embed_table.shape[1]
     s = rows // (2 * nx) // steps
+    block = 2 * nx * s
     far = max(nx - 1, 1)
     dma = pltpu.SemaphoreType.DMA
     return pl.pallas_call(
-        functools.partial(weights_kernel, nx, nz, steps),
-        out_shape=jax.ShapeDtypeStruct((rows, words), jnp.bfloat16),
-        in_specs=[pl.BlockSpec(memory_space=pl.ANY), pl.BlockSpec(memory_space=pltpu.VMEM)],
+        functools.partial(mixed_kernel, nx, nz, steps),
+        out_shape=jax.ShapeDtypeStruct((steps, block, width), jnp.bfloat16),
+        in_specs=[
+            pl.BlockSpec(memory_space=pl.ANY),
+            pl.BlockSpec(memory_space=pltpu.VMEM),
+            pl.BlockSpec(memory_space=pl.ANY),
+        ],
         out_specs=pl.BlockSpec(memory_space=pltpu.VMEM),
         scratch_shapes=[
             pltpu.VMEM((steps, nx, s, words), jnp.float32),
             pltpu.VMEM((steps, nx, s, words), jnp.float32),
             pltpu.VMEM((steps, far, s, words), jnp.float32),
+            pltpu.VMEM((steps, block, words), jnp.bfloat16),
+            pltpu.VMEM((words, width), jnp.bfloat16),
+            pltpu.VMEM((steps, block, width), jnp.bfloat16),
+            pltpu.VMEM((steps, nz - 1, block // nz, width), jnp.bfloat16),
             pltpu.VMEM((steps, s, 128), jnp.float32),
             pltpu.VMEM((steps, nz - 1, s, 128), jnp.float32),
+            dma,
             dma((steps, nx)), dma((steps, nx)), dma((steps, nx)),
             dma((steps, far)), dma((steps, far)),
             dma((steps, nz - 1)), dma((steps, nz - 1)),
             dma((steps,)), dma((steps,)),
             dma((steps, far)), dma((steps, far)),
             dma((steps, far)), dma((steps, far)),
+            dma((steps, nz - 1)), dma((steps, nz - 1)),
+            dma((steps, nz - 1)), dma((steps, nz - 1)),
         ],
         compiler_params=pltpu.CompilerParams(
             collective_id=0, has_side_effects=True, vmem_limit_bytes=VMEM_LIMIT
         ),
-        name="weights",
-    )(part, active)
-
-
-def embed_kernel(nz, parts, part_ref, out_ref, inbox, send, recv, out_send, out_recv):
-    z, zpeers = vocab_peers(nz)
-    rows = part_ref.shape[0] // nz
-    s = rows // parts
-    greet(zpeers)
-
-    def rows_of(owner, h):
-        return pl.ds(pl.multiple_of(owner * rows + h * s, s), s)
-
-    copies, gathers = {}, {}
-    for h in range(parts):
-        for d in range(1, nz):
-            copy = remote(part_ref.at[rows_of(lax.rem(z + d, nz), h)], inbox.at[h, d - 1],
-                          send.at[h, d - 1], recv.at[h, d - 1], zpeers[d - 1])
-            copy.start()
-            copies[h, d] = copy
-    for h in range(parts):
-        total = part_ref[rows_of(z, h), :].astype(jnp.float32)
-        for d in range(1, nz):
-            copies[h, d].wait_recv()
-            total = total + inbox[h, d - 1].astype(jnp.float32)
-        block = out_ref.at[rows_of(z, h)]
-        block[...] = total.astype(out_ref.dtype)
-        for d in range(1, nz):
-            copy = remote(block, block, out_send.at[h, d - 1], out_recv.at[h, d - 1], zpeers[d - 1])
-            copy.start()
-            gathers[h, d] = copy
-    for copy in gathers.values():
-        copy.wait_recv()
-    for copy in list(copies.values()) + list(gathers.values()):
-        copy.wait_send()
-
-
-def summed_embed(part, nz):
-    rows, columns = part.shape
-    parts = 2
-    s = rows // nz // parts
-    dma = pltpu.SemaphoreType.DMA
-    return pl.pallas_call(
-        functools.partial(embed_kernel, nz, parts),
-        out_shape=jax.ShapeDtypeStruct((rows, columns), jnp.bfloat16),
-        in_specs=[pl.BlockSpec(memory_space=pltpu.VMEM)],
-        out_specs=pl.BlockSpec(memory_space=pltpu.VMEM),
-        scratch_shapes=[
-            pltpu.VMEM((parts, nz - 1, s, columns), jnp.bfloat16),
-            dma((parts, nz - 1)), dma((parts, nz - 1)), dma((parts, nz - 1)), dma((parts, nz - 1)),
-        ],
-        compiler_params=pltpu.CompilerParams(
-            collective_id=1, has_side_effects=True, vmem_limit_bytes=VMEM_LIMIT
-        ),
-        name="embed_sum",
-    )(part)
+        name="expected_embedding",
+    )(part, active, embed_table)
 
 
 def qkv_kernel(nx, steps, part_ref, squares_ref, out_ref, core_buf, own_buf, chip_out, chip_in, squares_in,
@@ -253,8 +258,8 @@
         core_copies.append([])
         own_copies.append([])
         for d in list(range(1, nx)) + [0]:
-            there = pl.multiple_of((chip_at(d) * 2 + 1 - core) * own_rows + j * s, s)
-            here = pl.multiple_of((chip_at(d) * 2 + core) * own_rows + j * s, s)
+            there = pl.multiple_of(j * n * s + (chip_at(d) * 2 + 1 - core) * s, s)
+            here = pl.multiple_of(j * n * s + (chip_at(d) * 2 + core) * s, s)
             copy = remote(part_ref.at[pl.ds(there, s)], core_buf.at[j, d], core_send.at[j, d],
                           core_recv.at[j, d], partner)
             local = pltpu.make_async_copy(part_ref.at[pl.ds(here, s)], own_buf.at[j, d], own_sem.at[j, d])
@@ -264,7 +269,7 @@
             own_copies[j].append(local)
     sq_copies = []
     for i, other in enumerate(others):
-        block = squares_ref.at[pl.ds(pl.multiple_of(other * own_rows, own_rows), own_rows)]
+        block = squares_ref.at[:, other]
         copy = remote(block, squares_in.at[i], sq_send.at[i], sq_recv.at[i], {"req": other})
         copy.start()
         sq_copies.append(copy)
@@ -284,17 +289,17 @@
                 chip_copies[j, d] = copy
             else:
                 own_buf[j, 0] = total
-    squares = squares_ref[pl.ds(pl.multiple_of(me * own_rows, own_rows), own_rows), :]
+    squares = squares_ref[:, me]
     for i, copy in enumerate(sq_copies):
         copy.wait_recv()
         squares = squares + squares_in[i]
-    inv_rms = lax.rsqrt(squares[:, 0:1] / D + 1e-05)
+    inv_rms = lax.rsqrt(squares[:, :, 0:1] / D + 1e-05)
     for j in range(steps):
         total = own_buf[j, 0]
         for d in range(1, nx):
             chip_copies[j, d].wait_recv()
             total = total + chip_in[j, d - 1].astype(jnp.float32)
-        out_ref[j * s : (j + 1) * s, :] = (total * inv_rms[j * s : (j + 1) * s]).astype(out_ref.dtype)
+        out_ref[j * s : (j + 1) * s, :] = (total * inv_rms[j]).astype(out_ref.dtype)
     for j in range(steps):
         for copy in core_copies[j]:
             copy.wait_send()
@@ -304,7 +309,7 @@
 
 def scattered_qkv(part, squares, nx):
     rows, columns = part.shape
-    steps = 2
+    steps = squares.shape[0]
     own = rows // (2 * nx)
     s = own // steps
     far = max(nx - 1, 1)
@@ -319,7 +324,7 @@
             pltpu.VMEM((steps, nx, s, columns), jnp.float32),
             pltpu.VMEM((steps, far, s, columns), jnp.bfloat16),
             pltpu.VMEM((steps, far, s, columns), jnp.bfloat16),
-            pltpu.VMEM((2 * nx - 1, own, 128), jnp.float32),
+            pltpu.VMEM((2 * nx - 1, steps, s, 128), jnp.float32),
             dma((steps, nx)), dma((steps, nx)), dma((steps, nx)),
             dma((steps, far)), dma((steps, far)),
             dma((2 * nx - 1,)), dma((2 * nx - 1,)),
@@ -336,14 +341,19 @@
     state_rows = jnp.take(last_states, slot_request, axis=0)
     partial_logits = jnp.dot(state_rows, head_weight, preferred_element_type=jnp.float32)
     live = jnp.broadcast_to(active.astype(jnp.float32)[:, None], (rows, 128))
-    weights = gathered_weights(partial_logits, live, nx, nz)
-    partial_embed = jnp.dot(weights, embed_table, preferred_element_type=jnp.float32)
-    soft_embed = summed_embed(partial_embed.astype(jnp.bfloat16), nz)
-    widened = soft_embed.astype(jnp.float32)
+    own_rows = rows // (2 * nx)
+    steps = 4
+    while steps > 1 and (rows // steps // nz) % 16:
+        steps //= 2
+    s = own_rows // steps
+    blocks = expected_embedding(partial_logits, live, embed_table, nx, nz, steps)
+    widened = blocks.reshape(rows, -1).astype(jnp.float32)
     squares = jnp.broadcast_to(jnp.sum(widened * widened, axis=1)[:, None], (rows, 128))
     scaled = (widened * norm_gain.astype(jnp.float32)[None, :]).astype(jnp.bfloat16)
     partial_qkv = jnp.dot(scaled, qkv_weight, preferred_element_type=jnp.float32)
-    return (soft_embed, scattered_qkv(partial_qkv, squares, nx))
+    qkv_out = scattered_qkv(partial_qkv, squares.reshape(steps, 2 * nx, s, 128), nx)
+    soft_embed = blocks.reshape(steps, 2 * nx, s, -1).transpose(1, 0, 2, 3).reshape(rows, -1)
+    return (soft_embed, qkv_out)
 
 
 def solution(mesh):

time: 194 us -> 162 us (0.84)
  matrix products: 42.9 us -> 25.7 us
  Pallas kernels: 143 us -> 126 us
  other arithmetic: 1.07 us -> 3.29 us
    pallas_call x2 -> x1, Pallas kernels: 129 us -> 112 us  [expected_embedding(): pl.pallas_call(functools.partial(mixed_kernel, nx, nz, steps), out_shape=...]
    dot_general x1 -> x0, matrix products: 16.8 us -> none  [on_device(): jnp.dot(weights, embed_table, preferred_element_type=jnp.float32)]
where the time goes in v2:
time: 162 us
  Pallas kernels  126 us (78%)
  matrix products  25.7 us (16%)
  local copies, waits for them, and re-layouts  6.2 us (4%)
  other arithmetic  3.29 us (2%)
    pallas_call x1, Pallas kernels, expected_embedding(): pl.pallas_call(functools.partial(mixed_kernel, nx, nz, steps), out_shape=...  112 us
    dot_general x1, matrix products, on_device(): jnp.dot(state_rows, head_weight, preferred_element_type=jnp.float32)  17.3 us
    pallas_call x1, Pallas kernels, scattered_qkv(): pl.pallas_call(functools.partial(qkv_kernel, nx, steps), out_shape=jax.Sh...  13.6 us
    dot_general x1, matrix products, on_device(): jnp.dot(scaled, qkv_weight, preferred_element_type=jnp.float32)  8.44 us

profile of v2, /device:TPU:0, one launch (start us, length us, event | category | flops | bytes accessed | tf_op | source)
XLA Modules:
  0.0 161.9 jit_solution(253670965595081764)
XLA Ops:
  0.6 0.0 copy-start
  0.6 0.8 compare_select_fusion
  1.4 0.5 copy-done
  1.9 1.4 gather_fusion
  3.2 0.7 compare_and_fusion
  3.9 0.0 copy-start.4
  3.9 17.3 %fusion.1.part_ref = f32[256,8000]{1,0:T(8,128)} fusion(bf16[2048,8000]{0,1:T(8,128)(2,1)} %param.8, bf16[256,2048]{1,0:T(8,128)(2,1)S(1)} %gather_fusion, pred[256]{0:T(512)(128)(4,1)S(1)} %compare_and_fusion), kind=kOutput, calls=%fused_computation.4 | convolution fusion | flops 8389132288 | bytes 42008832 | tf_op jit(solution)/shard_map/dot_general | solution.py:342
  21.2 0.0 copy-done.4
  21.2 0.8 broadcast_in_dim.30.active_ref
  22.0 0.0 copy-start.3
  22.0 112.4 %expected_embedding.1 = bf16[4,64,2048]{2,1,0:T(8,128)(2,1)} custom-call(f32[256,8000]{1,0:T(8,128)} %fusion.1.part_ref, f32[256,128]{1,0:T(8,128)} %broadcast_in_dim.30.active_ref, bf16[8000,2048]{1,0:T(8,128)(2,1)} %embed_ref.1), custom_call_target="tpu_custom_call" | custom-call | tf_op jit(solution)/shard_map/expected_embedding/pallas_call | solution.py:211
  134.3 0.0 copy-done.3
  134.3 0.0 copy-start.1
  134.4 1.5 fusion
  135.9 0.0 copy-start.2
  135.9 8.4 %fusion.6.part_ref = f32[256,2560]{1,0:T(8,128)} fusion(bf16[256,2048]{1,0:T(8,128)(2,1)S(1)} %fusion, bf16[2048,2560]{1,0:T(8,128)(2,1)} %param.11), kind=kOutput, calls=%fused_computation.12 | convolution fusion | flops 2684354560 | bytes 14155776 | tf_op jit(solution)/shard_map/dot_general | solution.py:353
  144.4 0.0 copy-done.2
  144.4 0.3 multiply_reduce_fusion
  144.6 0.1 broadcast_in_dim.31
  144.7 0.8 broadcast_in_dim.32.squares_ref
  145.5 13.6 %qkv_sum.1 = bf16[64,2560]{1,0:T(8,128)(2,1)} custom-call(f32[256,2560]{1,0:T(8,128)} %fusion.6.part_ref, f32[4,4,16,128]{3,2,1,0:T(8,128)} %broadcast_in_dim.32.squares_ref), custom_call_target="tpu_custom_call" | custom-call | tf_op jit(solution)/shard_map/qkv_sum/pallas_call | solution.py:317
  159.1 1.0 copy.10
  160.2 1.7 %copy.13 = bf16[64,2560]{1,0:T(8,128)(2,1)} copy(bf16[64,2560]{1,0:T(8,128)(2,1)} %qkv_sum.1) | data formatting | bytes 655360
  161.9 0.0 copy-done.1
  (3 shorter events, 0.0 us)
Async XLA Ops:
  0.6 1.2 copy-start
  3.9 17.3 %copy-start.4 = (s32[256]{0:T(256)S(1)}, s32[256]{0:T(256)}, u32[]{:S(2)}) copy-start(s32[256]{0:T(256)} %param.12) | copy-start | bytes 3076
  22.0 112.4 %copy-start.3 = (bf16[2048]{0:T(1024)(128)(2,1)S(1)}, bf16[2048]{0:T(1024)(128)(2,1)}, u32[]{:S(2)}) copy-start(bf16[2048]{0:T(1024)(128)(2,1)} %param.10) | copy-start | bytes 12292
  134.3 27.5 %copy-start.1 = (bf16[256,2048]{1,0:T(8,128)(2,1)S(1)}, bf16[256,2048]{1,0:T(8,128)(2,1)}, u32[]{:S(2)}) copy-start(bf16[256,2048]{1,0:T(8,128)(2,1)} %param.7) | copy-start | bytes 3145732
  135.9 8.5 %copy-start.2 = (bf16[4,64,2048]{2,1,0:T(8,128)(2,1)S(1)}, bf16[4,64,2048]{2,1,0:T(8,128)(2,1)}, u32[]{:S(2)}) copy-start(bf16[4,64,2048]{2,1,0:T(8,128)(2,1)} %expected_embedding.1) | copy-start | bytes 3145732

commit v3 on v2

--- a/solution.py
+++ b/solution.py
@@ -53,7 +53,9 @@
     own_rows = part_ref.shape[0] // (2 * nx)
     s = own_rows // steps
     piece = 2 * nx * s // nz
-    tile = 256
+    halves = 2
+    half = table.shape[1] // halves
+    tile = min(512, half)
     lane = lax.broadcasted_iota(jnp.int32, (s, 128), 1)
     greet([partner] + [peer(d) for d in range(1, nx)] + zpeers)
 
@@ -149,30 +151,37 @@
         for d in range(1, nx):
             fwd_copies[j, d].wait_recv()
 
-        @pl.loop(0, table.shape[1] // tile)
-        def _(c):
-            columns = pl.ds(pl.multiple_of(c * tile, tile), tile)
-            mixed[j, :, columns] = jnp.dot(
-                weights[j], table[:, columns], preferred_element_type=jnp.float32
-            ).astype(mixed.dtype)
-
-        for d in range(1, nz):
-            copy = remote(mixed.at[j, piece_of(lax.rem(z + d, nz))], inbox.at[j, d - 1],
-                          mix_send.at[j, d - 1], mix_recv.at[j, d - 1], zpeers[d - 1])
-            copy.start()
-            mix_copies[j, d] = copy
+        for h in range(halves):
+
+            @pl.loop(h * half // tile, (h + 1) * half // tile)
+            def _(c):
+                columns = pl.ds(pl.multiple_of(c * tile, tile), tile)
+                mixed[j, :, columns] = jnp.dot(
+                    weights[j], table[:, columns], preferred_element_type=jnp.float32
+                ).astype(mixed.dtype)
+
+            columns = pl.ds(h * half, half)
+            for d in range(1, nz):
+                copy = remote(mixed.at[j, piece_of(lax.rem(z + d, nz)), columns],
+                              inbox.at[j, d - 1, :, columns],
+                              mix_send.at[j, h, d - 1], mix_recv.at[j, h, d - 1], zpeers[d - 1])
+                copy.start()
+                mix_copies[j, h, d] = copy
 
     def gather_mixed(j):
-        total = mixed[j, piece_of(z), :].astype(jnp.float32)
-        for d in range(1, nz):
-            mix_copies[j, d].wait_recv()
-            total = total + inbox[j, d - 1].astype(jnp.float32)
-        block = out_ref.at[j, piece_of(z)]
-        block[...] = total.astype(out_ref.dtype)
-        for d in range(1, nz):
-            copy = remote(block, block, out_send.at[j, d - 1], out_recv.at[j, d - 1], zpeers[d - 1])
-            copy.start()
-            out_copies[j, d] = copy
+        for h in range(halves):
+            columns = pl.ds(h * half, half)
+            total = mixed[j, piece_of(z), columns].astype(jnp.float32)
+            for d in range(1, nz):
+                mix_copies[j, h, d].wait_recv()
+                total = total + inbox[j, d - 1, :, columns].astype(jnp.float32)
+            block = out_ref.at[j, piece_of(z), columns]
+            block[...] = total.astype(out_ref.dtype)
+            for d in range(1, nz):
+                copy = remote(block, block, out_send.at[j, h, d - 1], out_recv.at[j, h, d - 1],
+                              zpeers[d - 1])
+                copy.start()
+                out_copies[j, h, d] = copy
 
     for t in range(min(2, steps)):
         reduce_cores(t)
@@ -186,9 +195,9 @@
         if t >= 1:
             forward(t - 1)
             mix(t - 1)
+    forward(steps - 1)
     if steps >= 2:
         gather_mixed(steps - 2)
-    forward(steps - 1)
     mix(steps - 1)
     gather_mixed(steps - 1)
     for copy in out_copies.values():
@@ -234,8 +243,8 @@
             dma((steps,)), dma((steps,)),
             dma((steps, far)), dma((steps, far)),
             dma((steps, far)), dma((steps, far)),
-            dma((steps, nz - 1)), dma((steps, nz - 1)),
-            dma((steps, nz - 1)), dma((steps, nz - 1)),
+            dma((steps, 2, nz - 1)), dma((steps, 2, nz - 1)),
+            dma((steps, 2, nz - 1)), dma((steps, 2, nz - 1)),
         ],
         compiler_params=pltpu.CompilerParams(
             collective_id=0, has_side_effects=True, vmem_limit_bytes=VMEM_LIMIT

time: 162 us -> 154 us (0.951)
  Pallas kernels: 126 us -> 118 us
    pallas_call x1, Pallas kernels: 112 us -> 104 us  [expected_embedding(): pl.pallas_call(functools.partial(mixed_kernel, nx, nz, steps), out_shape=...]
where the time goes in v3:
time: 154 us; the launch traced here: 153 us
  Pallas kernels  118 us (77%)
  matrix products  25.7 us (17%)
  local copies, waits for them, and re-layouts  6.2 us (4%)
  other arithmetic  3.29 us (2%)
    pallas_call x1, Pallas kernels, expected_embedding(): pl.pallas_call(functools.partial(mixed_kernel, nx, nz, steps), out_shape=...  104 us
    dot_general x1, matrix products, on_device(): jnp.dot(state_rows, head_weight, preferred_element_type=jnp.float32)  17.3 us
    pallas_call x1, Pallas kernels, scattered_qkv(): pl.pallas_call(functools.partial(qkv_kernel, nx, steps), out_shape=jax.Sh...  13.6 us
    dot_general x1, matrix products, on_device(): jnp.dot(scaled, qkv_weight, preferred_element_type=jnp.float32)  8.44 us

profile of v3, /device:TPU:0, one launch (start us, length us, event | category | flops | bytes accessed | tf_op | source)
XLA Modules:
  0.0 153.4 jit_solution(16049225142325195882)
XLA Ops:
  0.6 0.0 copy-start
  0.6 0.8 compare_select_fusion
  1.4 0.5 copy-done
  1.9 1.4 gather_fusion
  3.2 0.7 compare_and_fusion
  3.9 0.0 copy-start.4
  3.9 17.3 %fusion.1.part_ref = f32[256,8000]{1,0:T(8,128)} fusion(bf16[2048,8000]{0,1:T(8,128)(2,1)} %param.8, bf16[256,2048]{1,0:T(8,128)(2,1)S(1)} %gather_fusion, pred[256]{0:T(512)(128)(4,1)S(1)} %compare_and_fusion), kind=kOutput, calls=%fused_computation.4 | convolution fusion | flops 8389132288 | bytes 42008832 | tf_op jit(solution)/shard_map/dot_general | solution.py:351
  21.2 0.0 copy-done.4
  21.2 0.8 broadcast_in_dim.30.active_ref
  22.0 0.0 copy-start.3
  22.0 103.9 %expected_embedding.1 = bf16[4,64,2048]{2,1,0:T(8,128)(2,1)} custom-call(f32[256,8000]{1,0:T(8,128)} %fusion.1.part_ref, f32[256,128]{1,0:T(8,128)} %broadcast_in_dim.30.active_ref, bf16[8000,2048]{1,0:T(8,128)(2,1)} %embed_ref.1), custom_call_target="tpu_custom_call" | custom-call | tf_op jit(solution)/shard_map/expected_embedding/pallas_call | solution.py:220
  125.8 0.0 copy-done.3
  125.8 0.0 copy-start.1
  125.9 1.5 fusion
  127.4 0.0 copy-start.2
  127.4 8.4 %fusion.6.part_ref = f32[256,2560]{1,0:T(8,128)} fusion(bf16[256,2048]{1,0:T(8,128)(2,1)S(1)} %fusion, bf16[2048,2560]{1,0:T(8,128)(2,1)} %param.11), kind=kOutput, calls=%fused_computation.12 | convolution fusion | flops 2684354560 | bytes 14155776 | tf_op jit(solution)/shard_map/dot_general | solution.py:362
  135.9 0.0 copy-done.2
  135.9 0.3 multiply_reduce_fusion
  136.1 0.1 broadcast_in_dim.31
  136.2 0.8 broadcast_in_dim.32.squares_ref
  137.0 13.6 %qkv_sum.1 = bf16[64,2560]{1,0:T(8,128)(2,1)} custom-call(f32[256,2560]{1,0:T(8,128)} %fusion.6.part_ref, f32[4,4,16,128]{3,2,1,0:T(8,128)} %broadcast_in_dim.32.squares_ref), custom_call_target="tpu_custom_call" | custom-call | tf_op jit(solution)/shard_map/qkv_sum/pallas_call | solution.py:326
  150.6 1.0 copy.10
  151.7 1.7 %copy.13 = bf16[64,2560]{1,0:T(8,128)(2,1)} copy(bf16[64,2560]{1,0:T(8,128)(2,1)} %qkv_sum.1) | data formatting | bytes 655360
  153.4 0.0 copy-done.1
  (3 shorter events, 0.0 us)
Async XLA Ops:
  0.6 1.2 copy-start
  3.9 17.3 %copy-start.4 = (s32[256]{0:T(256)S(1)}, s32[256]{0:T(256)}, u32[]{:S(2)}) copy-start(s32[256]{0:T(256)} %param.12) | copy-start | bytes 3076
  22.0 103.9 %copy-start.3 = (bf16[2048]{0:T(1024)(128)(2,1)S(1)}, bf16[2048]{0:T(1024)(128)(2,1)}, u32[]{:S(2)}) copy-start(bf16[2048]{0:T(1024)(128)(2,1)} %param.10) | copy-start | bytes 12292
  125.8 27.5 %copy-start.1 = (bf16[256,2048]{1,0:T(8,128)(2,1)S(1)}, bf16[256,2048]{1,0:T(8,128)(2,1)}, u32[]{:S(2)}) copy-start(bf16[256,2048]{1,0:T(8,128)(2,1)} %param.7) | copy-start | bytes 3145732
  127.4 8.5 %copy-start.2 = (bf16[4,64,2048]{2,1,0:T(8,128)(2,1)S(1)}, bf16[4,64,2048]{2,1,0:T(8,128)(2,1)}, u32[]{:S(2)}) copy-start(bf16[4,64,2048]{2,1,0:T(8,128)(2,1)} %expected_embedding.1) | copy-start | bytes 3145732
